TPU v7x, 32 devices: a whole 2x2x4 slice. The times are simulated.
32 devices in a mesh: graph: 8 (over z, x), dp: 4 (over y, core).
Axes of the slice: x: 2, y: 2, z: 4, core: 2. Of those that a mesh axis runs over, the one named last changes fastest.
Arguments:
- node_state: bfloat16 [4, 4096, 512], P('dp', 'graph'), may hold values from -6 to 6
- edge_state: bfloat16 [4, 16384, 512], P('dp', 'graph'), may hold values from -6 to 6
- senders: int32 [4, 16384], P('dp', 'graph'), may hold values from 0 to 575
- receivers: int32 [4, 16384], P('dp', 'graph'), may hold values from 0 to 511
- send_index: int32 [4, 8, 64], P('dp', 'graph'), may hold values from 0 to 511
- cotangent: bfloat16 [4, 4096, 512], P('dp', 'graph'), may hold values from -0.09375 to 0.09375
- w_edge: bfloat16 [1536, 512], replicated, may hold values from -0.15625 to 0.15625
- w_node: bfloat16 [1024, 512], replicated, may hold values from -0.1875 to 0.1875
- error_memory: float32 [4, 1024, 512], P('dp', 'graph'), may hold values from -6 to 6
- warm_q: float32 [512, 64], replicated, may hold values from -6 to 6
Outputs:
- new_nodes: bfloat16 [4, 4096, 512], P('dp', 'graph')
- update: float32 [1024, 512], P('graph')
- new_error: float32 [4, 1024, 512], P('dp', 'graph')
- new_q: float32 [512, 64], replicated
All inputs are finite; a program needn't handle non-finite values.
Results may differ from a plain program's by a relative error of at most 0.0066.
Values may be sent and summed in bfloat16 or wider, within the bound.
No kernel may reach another device: no remote copies, remote signals or barrier semaphores. Data moves between devices by JAX's collectives and lax.ppermute only.
A program may use at most 64 MiB of HBM per device.

v0:
```python
import jax
import jax.numpy as jnp
from jax import lax
from jax.sharding import PartitionSpec as P


def silu_slope(pre_act):
    sigmoid_v = jax.nn.sigmoid(pre_act)
    return sigmoid_v * (1.0 + pre_act * (1.0 - sigmoid_v))


def body(
    node_state,
    edge_state,
    senders,
    receivers,
    send_index,
    cotangent,
    w_edge,
    w_node,
    error_memory,
    warm_q,
):
    highest = lax.Precision.HIGHEST
    node_block = node_state[0]
    edge_block = edge_state[0]
    features = node_block.shape[1]
    node_count = node_block.shape[0]
    partitions = lax.axis_size("graph")
    outgoing = node_block[send_index[0, 0]].reshape(partitions, -1, features)
    incoming = lax.all_to_all(outgoing, "graph", split_axis=0, concat_axis=0, tiled=True)
    lookup = jnp.concatenate([node_block, incoming.reshape(-1, features)], axis=0)
    sender_rows = lookup[senders[0]]
    receiver_rows = node_block[receivers[0]]
    edge_pre = jnp.dot(edge_block, w_edge[:features], preferred_element_type=jnp.float32)
    edge_pre = edge_pre + jnp.dot(
        sender_rows, w_edge[features : 2 * features], preferred_element_type=jnp.float32
    )
    edge_pre = edge_pre + jnp.dot(
        receiver_rows, w_edge[2 * features :], preferred_element_type=jnp.float32
    )
    edge_new = (edge_block.astype(jnp.float32) + jax.nn.silu(edge_pre)).astype(jnp.bfloat16)
    incidence = (receivers[0][None, :] == jnp.arange(node_count, dtype=jnp.int32)[:, None]).astype(
        jnp.bfloat16
    )
    aggregate = jnp.dot(incidence, edge_new, preferred_element_type=jnp.float32).astype(
        jnp.bfloat16
    )
    node_pre = jnp.dot(node_block, w_node[:features], preferred_element_type=jnp.float32)
    node_pre = node_pre + jnp.dot(aggregate, w_node[features:], preferred_element_type=jnp.float32)
    new_block = (node_block.astype(jnp.float32) + jax.nn.silu(node_pre)).astype(jnp.bfloat16)
    node_delta = (cotangent[0].astype(jnp.float32) * silu_slope(node_pre)).astype(jnp.bfloat16)
    grad_top = jnp.einsum("nk,nj->kj", node_block, node_delta, preferred_element_type=jnp.float32)
    grad_low = jnp.einsum("nk,nj->kj", aggregate, node_delta, preferred_element_type=jnp.float32)
    gradient = jnp.concatenate([grad_top, grad_low], axis=0)
    mine = lax.psum_scatter(gradient, "graph", scatter_dimension=0, tiled=True)
    matrix = mine + error_memory[0]
    local_left = jnp.dot(matrix, warm_q, precision=highest)
    own_left = lax.psum(local_left, "dp")
    gram = lax.psum(jnp.dot(own_left.T, own_left, precision=highest), "graph")
    factor = jnp.linalg.cholesky(gram)
    ortho = lax.linalg.triangular_solve(
        factor, own_left, left_side=False, lower=True, transpose_a=True
    )
    right_part = jnp.dot(matrix.T, ortho, precision=highest)
    new_q = lax.psum(right_part, ("graph", "dp")) / lax.axis_size("dp")
    update = jnp.dot(ortho, new_q.T, precision=highest)
    new_error = matrix - update
    return (new_block[None], update, new_error[None], new_q)


def solution(mesh):
    return jax.shard_map(
        body,
        mesh=mesh,
        in_specs=(
            P("dp", "graph", None),
            P("dp", "graph", None),
            P("dp", "graph"),
            P("dp", "graph"),
            P("dp", "graph", None),
            P("dp", "graph", None),
            P(),
            P(),
            P("dp", "graph", None),
            P(),
        ),
        out_specs=(P("dp", "graph", None), P("graph", None), P("dp", "graph", None), P()),
        check_vma=False,
    )
```

profile of v0, /device:TPU:0, one launch (start us, length us, event | category | flops | bytes accessed | tf_op | source)
XLA Modules:
  0.0 321.9 jit_solution(285913944859563682)
XLA Ops:
  7.2 0.7 fusion.19
  7.9 2.4 gather_fusion
  10.4 7.3 %all-to-all-start = ((bf16[8,8,512]{2,1,0:T(8,128)(2,1)}), bf16[8,8,512]{2,1,0:T(8,128)(2,1)S(1)}, u32[]{:S(2)}, u32[]{:S(2)}) async-start(bf16[8,8,512]{2,1,0:T(8,128)(2,1)} %bitcast.5), calls=%async_computation | async-start | bytes 131072 | tf_op jit(solution)/shard_map/all_to_all | solution.py:31
  17.7 0.7 compare_select_fusion.1
  18.4 0.7 compare_select_fusion
  19.2 9.2 %gather_fusion.2 = bf16[2048,512]{1,0:T(8,128)(2,1)} fusion(bf16[512,512]{1,0:T(8,128)(2,1)S(1)} %bitcast.63, s32[2048]{0:T(1024)S(1)} %broadcast_clamp_fusion), kind=kCustom, calls=%fused_computation.2 | custom fusion | bytes 4202496 | tf_op jit(solution)/shard_map/gather | solution.py:34
  28.4 1.4 fusion.12
  29.8 0.6 copy-done.2
  30.3 4.3 %fusion.1 = f32[2048,512]{1,0:T(8,128)} fusion(bf16[1,2048,512]{2,1,0:T(8,128)(2,1)S(1)} %copy-done.2, bf16[1536,512]{1,0:T(8,128)(2,1)} %param.16), kind=kOutput, calls=%fused_computation.7 | convolution fusion | flops 1073741824 | bytes 6815744 | tf_op jit(solution)/shard_map/dot_general | solution.py:35
  34.6 7.5 %gather_fusion.1 = bf16[2048,512]{1,0:T(8,128)(2,1)S(1)} fusion(bf16[576,512]{1,0:T(8,128)(2,1)S(1)} %pad_maximum_fusion.1, s32[2048]{0:T(1024)S(1)} %broadcast_clamp_fusion.1), kind=kCustom, calls=%fused_computation.1 | custom fusion | bytes 4202496 | tf_op jit(solution)/shard_map/gather | solution.py:33
  42.2 4.3 %fusion.9 = f32[2048,512]{1,0:T(8,128)} fusion(bf16[2048,512]{1,0:T(8,128)(2,1)S(1)} %gather_fusion.1, bf16[1536,512]{1,0:T(8,128)(2,1)} %param.16), kind=kOutput, calls=%fused_computation.20 | convolution fusion | flops 1073741824 | bytes 6815744 | tf_op jit(solution)/shard_map/dot_general | solution.py:36
  46.5 8.2 %fusion.4 = bf16[512,512]{1,0:T(8,128)(2,1)S(1)} fusion(s32[2048]{0:T(1024)S(1)} %bitcast.68, f32[2048,512]{1,0:T(8,128)} %fusion.1, f32[2048,512]{1,0:T(8,128)} %fusion.9, bf16[2048,512]{1,0:T(8,128)(2,1)} %gather_fusion.2, bf16[1,2048,512]{2,1,0:T(8,128)(2,1)} %param.11, bf16[1536,512]{1,0:T(8,128)(2,1)} %param.16), kind=kOutput, calls=%fused_computation.12 | convolution fusion | flops 2158231552 | bytes 13639680 | tf_op jit(solution)/shard_map/dot_general | solution.py:46
  54.7 2.7 fusion.5
  57.4 0.5 fusion.27
  57.8 0.5 convolution_bitcast_fusion
  58.3 1.5 pad_maximum_fusion
  59.9 69.8 %reduce-scatter.2.cloned.1.call-done = f32[128,512]{1,0:T(8,128)} async-done(((f32[1024,512]{1,0:T(8,128)}), f32[128,512]{1,0:T(8,128)}) %reduce-scatter.2.cloned.1.call-update) | async-done | bytes 262160 | tf_op jit(solution)/shard_map/reduce_scatter | solution.py:56
  129.8 1.4 fusion.24
  131.2 10.3 %psum.21 = f32[128,64]{0,1:T(8,128)S(1)} all-reduce(f32[128,64]{0,1:T(8,128)S(1)} %fusion.24), channel_id=1, replica_groups=mesh['graph'=8,'dp'=4] {'dp'}, use_global_device_ids=true, to_apply=%region_1.2 | all-reduce | flops 8192 | bytes 65536 | tf_op jit(solution)/shard_map/psum | solution.py:59
  141.4 0.2 fusion.28
  141.6 34.8 %psum.22 = f32[64,64]{0,1:T(8,128)S(1)} all-reduce(f32[64,64]{0,1:T(8,128)S(1)} %fusion.28), channel_id=1, replica_groups=mesh['graph'=8,'dp'=4] {'graph'}, use_global_device_ids=true, to_apply=%region_2.3 | all-reduce | flops 4096 | bytes 32768 | tf_op jit(solution)/shard_map/psum | solution.py:60
  176.5 0.1 copy.17
  176.6 5.9 %cholesky.16 = f32[64,64]{1,0:T(8,128)S(1)} custom-call(f32[64,64]{1,0:T(8,128)S(1)} %fusion.18), custom_call_target="Cholesky" | custom-call | tf_op jit(solution)/shard_map/jit(cholesky)/cholesky | solution.py:61
  182.5 0.6 compare_reduce_fusion
  183.1 0.7 fusion.15
  183.8 4.9 %custom-call.6 = f32[1,64,64]{1,2,0:T(8,128)S(1)} custom-call(f32[1,64,64]{2,1,0:T(8,128)S(1)} %fusion.15), custom_call_target="InvertDiagBlocksLowerTriangular" | custom-call | tf_op jit(solution)/shard_map/triangular_solve | solution.py:62
  188.7 0.2 fusion.16
  188.9 1.9 fusion.23
  190.8 122.1 %all-reduce.2.cloned.1.call-done = f32[512,64]{0,1:T(8,128)} async-done(((f32[512,64]{0,1:T(8,128)}), f32[512,64]{0,1:T(8,128)}) %all-reduce.2.cloned.1.call-update) | async-done | bytes 131088 | tf_op jit(solution)/shard_map/psum | solution.py:66
  312.9 0.9 broadcast_multiply_fusion
  313.8 0.4 fusion.29
  314.3 0.8 subtract_bitcast_fusion
  (32 shorter events, 0.3 us)
Async XLA Ops:
  7.2 122.6 %copy-start = (f32[512,64]{0,1:T(8,128)S(1)}, f32[512,64]{0,1:T(8,128)}, u32[]{:S(2)}) copy-start(f32[512,64]{0,1:T(8,128)} %param.19) | copy-start | bytes 393220
  7.2 12.0 %copy-start.1 = (bf16[1,512,512]{2,1,0:T(8,128)(2,1)S(1)}, bf16[1,512,512]{2,1,0:T(8,128)(2,1)}, u32[]{:S(2)}) copy-start(bf16[1,512,512]{2,1,0:T(8,128)(2,1)} %param.10) | copy-start | bytes 1572868
  10.4 24.2 %all-to-all-start = ((bf16[8,8,512]{2,1,0:T(8,128)(2,1)}), bf16[8,8,512]{2,1,0:T(8,128)(2,1)S(1)}, u32[]{:S(2)}, u32[]{:S(2)}) async-start(bf16[8,8,512]{2,1,0:T(8,128)(2,1)} %bitcast.5), calls=%async_computation | async-start | bytes 131072 | tf_op jit(solution)/shard_map/all_to_all | solution.py:31
  17.7 112.1 %reduce-scatter.2.cloned.1.call-start = ((), (), s32[]{:S(2)}) async-start(), calls=%async_computation.2 | async-start | bytes 2359296 | tf_op jit(solution)/shard_map/reduce_scatter | solution.py:56
  19.1 9.2 %copy-start.8 = (bf16[1024,512]{1,0:T(8,128)(2,1)S(1)}, bf16[1024,512]{1,0:T(8,128)(2,1)}, u32[]{:S(2)}) copy-start(bf16[1024,512]{1,0:T(8,128)(2,1)} %param.17) | copy-start | bytes 3145732
  28.4 2.0 copy-start.2
  42.2 4.3 %copy-start.10 = (s32[1,2048]{1,0:T(1,128)S(1)}, s32[1,2048]{1,0:T(1,128)}, u32[]{:S(2)}) copy-start(s32[1,2048]{1,0:T(1,128)} %param.13) | copy-start | bytes 24580
  46.5 8.2 %copy-start.5 = (f32[512,512]{1,0:T(8,128)S(1)}, f32[512,512]{1,0:T(8,128)}, u32[]{:S(2)}) copy-start(f32[512,512]{1,0:T(8,128)} %fusion.12) | copy-start | bytes 3145732
  46.5 8.2 %copy-start.9 = (bf16[1024,512]{1,0:T(8,128)(2,1)S(1)}, bf16[1024,512]{1,0:T(8,128)(2,1)}, u32[]{:S(2)}) copy-start(bf16[1024,512]{1,0:T(8,128)(2,1)} %param.17) | copy-start | bytes 3145732
  59.8 69.9 %copy-start.3 = (f32[1,128,512]{2,1,0:T(8,128)S(1)}, f32[1,128,512]{2,1,0:T(8,128)}, u32[]{:S(2)}) copy-start(f32[1,128,512]{2,1,0:T(8,128)} %param.18) | copy-start | bytes 786436
  59.9 253.0 %all-reduce.2.cloned.1.call-start = ((), (), s32[]{:S(2)}) async-start(), calls=%async_computation.3 | async-start | bytes 262144 | tf_op jit(solution)/shard_map/psum | solution.py:66
  129.7 184.5 %copy-start.4 = (f32[128,512]{1,0:T(8,128)S(1)}, f32[128,512]{1,0:T(8,128)}, u32[]{:S(2)}) copy-start(f32[128,512]{1,0:T(8,128)} %reduce-scatter.2.cloned.1.call-done) | copy-start | bytes 786436
  313.8 1.2 copy-start.7
  314.3 0.8 copy-start.6
Sparse Core Ops, SparseCore 0:
  60.0 69.7 reduce-scatter.1
  191.0 121.8 all-reduce.1
where the time goes:
time: 322 us
  waiting for transfers between devices  192 us (60%)
  blocking collectives  45.1 us (14%)
  matrix products  25.9 us (8%)
  local copies, waits for them, and re-layouts  19.9 us (6%)
  other arithmetic  17.5 us (5%)
  between operations  14.2 us (4%)
  starting transfers between devices  7.36 us (2%)
    psum x1, waiting for transfers between devices, body(): new_q = lax.psum(right_part, ('graph', 'dp')) / lax.axis_size('dp')  122 us
    reduce_scatter x1, waiting for transfers between devices, body(): mine = lax.psum_scatter(gradient, 'graph', scatter_dimension=0, tiled=True)  69.8 us
    psum x1, blocking collectives, body(): gram = lax.psum(jnp.dot(own_left.T, own_left, precision=highest), 'graph')  34.8 us
    psum x1, blocking collectives, body(): own_left = lax.psum(local_left, 'dp')  10.3 us
    gather x1, local copies, waits for them, and re-layouts, body(): receiver_rows = node_block[receivers[0]]  9.2 us
    dot_general x1, matrix products, body(): jnp.dot(incidence, edge_new, preferred_element_type=jnp.float32)  8.16 us
    gather x1, local copies, waits for them, and re-layouts, body(): sender_rows = lookup[senders[0]]  7.54 us
    all_to_all x1, starting transfers between devices, body(): lax.all_to_all(outgoing, 'graph', split_axis=0, concat_axis=0, tiled=True)  7.28 us
  transfers between devices with their start and end apart: 3, of which 2 were waited for; matrix products, arithmetic and copies ran while one was open for 5% of the time, Pallas kernels for 0%

commit v1 on v0

--- a/solution.py
+++ b/solution.py
@@ -63,7 +63,7 @@
         factor, own_left, left_side=False, lower=True, transpose_a=True
     )
     right_part = jnp.dot(matrix.T, ortho, precision=highest)
-    new_q = lax.psum(right_part, ("graph", "dp")) / lax.axis_size("dp")
+    new_q = jnp.sum(lax.all_gather(right_part, ("graph", "dp")), axis=0) / lax.axis_size("dp")
     update = jnp.dot(ortho, new_q.T, precision=highest)
     new_error = matrix - update
     return (new_block[None], update, new_error[None], new_q)

time: 322 us -> 264 us (0.82)
  waiting for transfers between devices: 192 us -> 129 us
  local copies, waits for them, and re-layouts: 19.9 us -> 24.4 us
    psum x1 -> x0, waiting for transfers between devices: 122 us -> none  [body(): new_q = lax.psum(right_part, ('graph', 'dp')) / lax.axis_size('dp')]
    all_gather x0 -> x1, waiting for transfers between devices: none -> 59.3 us  [body(): lax.all_gather(right_part, ('graph', 'dp'))]
    unnamed x22 -> x23, local copies, waits for them, and re-layouts: 0.62 us -> 5.18 us
  transfers between devices with their start and end apart: 3 -> 3, of which waited for: 2 -> 2; matrix products, arithmetic and copies ran while one was open for 5% -> 6% of each run, Pallas kernels for 0% -> 0%
where the time goes in v1:
time: 264 us; the launch traced here: 263 us
  waiting for transfers between devices  129 us (49%)
  blocking collectives  45.2 us (17%)
  matrix products  25.9 us (10%)
  local copies, waits for them, and re-layouts  24.4 us (9%)
  other arithmetic  17.2 us (7%)
  between operations  14.3 us (5%)
  starting transfers between devices  7.36 us (3%)
    reduce_scatter x1, waiting for transfers between devices, body(): mine = lax.psum_scatter(gradient, 'graph', scatter_dimension=0, tiled=True)  69.8 us
    all_gather x1, waiting for transfers between devices, body(): lax.all_gather(right_part, ('graph', 'dp'))  59.3 us
    psum x1, blocking collectives, body(): gram = lax.psum(jnp.dot(own_left.T, own_left, precision=highest), 'graph')  34.9 us
    psum x1, blocking collectives, body(): own_left = lax.psum(local_left, 'dp')  10.3 us
    gather x1, local copies, waits for them, and re-layouts, body(): receiver_rows = node_block[receivers[0]]  9.2 us
    dot_general x1, matrix products, body(): jnp.dot(incidence, edge_new, preferred_element_type=jnp.float32)  8.16 us
    gather x1, local copies, waits for them, and re-layouts, body(): sender_rows = lookup[senders[0]]  7.54 us
    all_to_all x1, starting transfers between devices, body(): lax.all_to_all(outgoing, 'graph', split_axis=0, concat_axis=0, tiled=True)  7.28 us
  transfers between devices with their start and end apart: 3, of which 2 were waited for; matrix products, arithmetic and copies ran while one was open for 6% of the time, Pallas kernels for 0%

profile of v1, /device:TPU:0, one launch (start us, length us, event | category | flops | bytes accessed | tf_op | source)
XLA Modules:
  0.0 263.5 jit_solution(6957827848926175311)
XLA Ops:
  7.2 0.7 fusion.19
  7.9 2.4 gather_fusion
  10.4 7.3 %all-to-all-start = ((bf16[8,8,512]{2,1,0:T(8,128)(2,1)}), bf16[8,8,512]{2,1,0:T(8,128)(2,1)S(1)}, u32[]{:S(2)}, u32[]{:S(2)}) async-start(bf16[8,8,512]{2,1,0:T(8,128)(2,1)} %bitcast.5), calls=%async_computation | async-start | bytes 131072 | tf_op jit(solution)/shard_map/all_to_all | solution.py:31
  17.7 0.7 compare_select_fusion.1
  18.4 0.7 compare_select_fusion
  19.2 9.2 %gather_fusion.2 = bf16[2048,512]{1,0:T(8,128)(2,1)} fusion(bf16[512,512]{1,0:T(8,128)(2,1)S(1)} %bitcast.68, s32[2048]{0:T(1024)S(1)} %broadcast_clamp_fusion), kind=kCustom, calls=%fused_computation.2 | custom fusion | bytes 4202496 | tf_op jit(solution)/shard_map/gather | solution.py:34
  28.4 1.4 fusion.12
  29.8 0.6 copy-done.2
  30.3 4.3 %fusion.1 = f32[2048,512]{1,0:T(8,128)} fusion(bf16[1,2048,512]{2,1,0:T(8,128)(2,1)S(1)} %copy-done.2, bf16[1536,512]{1,0:T(8,128)(2,1)} %param.16), kind=kOutput, calls=%fused_computation.8 | convolution fusion | flops 1073741824 | bytes 6815744 | tf_op jit(solution)/shard_map/dot_general | solution.py:35
  34.6 7.5 %gather_fusion.1 = bf16[2048,512]{1,0:T(8,128)(2,1)S(1)} fusion(bf16[576,512]{1,0:T(8,128)(2,1)S(1)} %pad_maximum_fusion.1, s32[2048]{0:T(1024)S(1)} %broadcast_clamp_fusion.1), kind=kCustom, calls=%fused_computation.1 | custom fusion | bytes 4202496 | tf_op jit(solution)/shard_map/gather | solution.py:33
  42.2 4.3 %fusion.9 = f32[2048,512]{1,0:T(8,128)} fusion(bf16[2048,512]{1,0:T(8,128)(2,1)S(1)} %gather_fusion.1, bf16[1536,512]{1,0:T(8,128)(2,1)} %param.16), kind=kOutput, calls=%fused_computation.21 | convolution fusion | flops 1073741824 | bytes 6815744 | tf_op jit(solution)/shard_map/dot_general | solution.py:36
  46.5 8.2 %fusion.4 = bf16[512,512]{1,0:T(8,128)(2,1)S(1)} fusion(s32[2048]{0:T(1024)S(1)} %bitcast.74, f32[2048,512]{1,0:T(8,128)} %fusion.1, f32[2048,512]{1,0:T(8,128)} %fusion.9, bf16[2048,512]{1,0:T(8,128)(2,1)} %gather_fusion.2, bf16[1,2048,512]{2,1,0:T(8,128)(2,1)} %param.11, bf16[1536,512]{1,0:T(8,128)(2,1)} %param.16), kind=kOutput, calls=%fused_computation.13 | convolution fusion | flops 2158231552 | bytes 13639680 | tf_op jit(solution)/shard_map/dot_general | solution.py:46
  54.7 2.7 %fusion.5 = (bf16[512,512]{1,0:T(8,128)(2,1)S(1)}, bf16[1,512,512]{2,1,0:T(8,128)(2,1)}) fusion(bf16[1,512,512]{2,1,0:T(8,128)(2,1)} %param.15, bf16[1,512,512]{2,1,0:T(8,128)(2,1)S(1)} %copy-done.1, f32[512,512]{1,0:T(8,128)S(1)} %copy-done.5, bf16[512,512]{1,0:T(8,128)(2,1)S(1)} %fusion.4, bf16[1024,512]{1,0:T(8,128)(2,1)S(1)} %copy-done.9), kind=kOutput, calls=%fused_computation.15 | convolution fusion | flops 272367616 | bytes 4194304 | tf_op jit(solution)/shard_map/dot_general | solution.py:50
  57.4 0.5 fusion.27
  57.8 0.5 convolution_bitcast_fusion
  58.3 1.5 pad_maximum_fusion
  59.9 69.8 %reduce-scatter.2.cloned.1.call-done = f32[128,512]{1,0:T(8,128)} async-done(((f32[1024,512]{1,0:T(8,128)}), f32[128,512]{1,0:T(8,128)}) %reduce-scatter.2.cloned.1.call-update) | async-done | bytes 262160 | tf_op jit(solution)/shard_map/reduce_scatter | solution.py:56
  129.7 1.3 fusion.24
  131.1 10.3 %psum.14 = f32[128,64]{0,1:T(8,128)S(1)} all-reduce(f32[128,64]{0,1:T(8,128)S(1)} %fusion.24), channel_id=1, replica_groups=mesh['graph'=8,'dp'=4] {'dp'}, use_global_device_ids=true, to_apply=%region_1.2 | all-reduce | flops 8192 | bytes 65536 | tf_op jit(solution)/shard_map/psum | solution.py:59
  141.3 0.2 fusion.28
  141.5 34.9 %psum.15 = f32[64,64]{0,1:T(8,128)S(1)} all-reduce(f32[64,64]{0,1:T(8,128)S(1)} %fusion.28), channel_id=1, replica_groups=mesh['graph'=8,'dp'=4] {'graph'}, use_global_device_ids=true, to_apply=%region_2.3 | all-reduce | flops 4096 | bytes 32768 | tf_op jit(solution)/shard_map/psum | solution.py:60
  176.5 5.8 %cholesky.16 = f32[64,64]{1,0:T(8,128)S(1)} custom-call(f32[64,64]{1,0:T(8,128)S(1)} %fusion.18), custom_call_target="Cholesky" | custom-call | tf_op jit(solution)/shard_map/jit(cholesky)/cholesky | solution.py:61
  182.4 0.6 compare_reduce_fusion
  183.1 0.7 fusion.15
  183.7 4.9 %custom-call.6 = f32[1,64,64]{1,2,0:T(8,128)S(1)} custom-call(f32[1,64,64]{2,1,0:T(8,128)S(1)} %fusion.15), custom_call_target="InvertDiagBlocksLowerTriangular" | custom-call | tf_op jit(solution)/shard_map/triangular_solve | solution.py:62
  188.6 0.3 fusion.16
  188.9 1.9 fusion.23
  190.8 59.3 %all-gather.3.cloned.1.call-done = f32[16384,64]{0,1:T(8,128)} async-done(((f32[512,64]{0,1:T(8,128)}), f32[16384,64]{0,1:T(8,128)}) %all-gather.3.cloned.1.call-update) | async-done | bytes 4194320 | tf_op jit(solution)/shard_map/all_gather | solution.py:66
  250.1 4.6 %copy.19 = f32[8,8,32,512]{3,2,1,0:T(8,128)S(1)} copy(f32[8,8,32,512]{3,1,2,0:T(8,128)} %bitcast.70) | data formatting | bytes 8388608
  254.7 0.7 bitcast_reduce_fusion
  255.4 0.4 fusion.29
  255.8 0.8 subtract_bitcast_fusion
  (34 shorter events, 0.4 us)
Async XLA Ops:
  7.2 122.5 %copy-start = (f32[512,64]{0,1:T(8,128)S(1)}, f32[512,64]{0,1:T(8,128)}, u32[]{:S(2)}) copy-start(f32[512,64]{0,1:T(8,128)} %param.19) | copy-start | bytes 393220
  7.2 12.0 %copy-start.1 = (bf16[1,512,512]{2,1,0:T(8,128)(2,1)S(1)}, bf16[1,512,512]{2,1,0:T(8,128)(2,1)}, u32[]{:S(2)}) copy-start(bf16[1,512,512]{2,1,0:T(8,128)(2,1)} %param.10) | copy-start | bytes 1572868
  10.4 24.2 %all-to-all-start = ((bf16[8,8,512]{2,1,0:T(8,128)(2,1)}), bf16[8,8,512]{2,1,0:T(8,128)(2,1)S(1)}, u32[]{:S(2)}, u32[]{:S(2)}) async-start(bf16[8,8,512]{2,1,0:T(8,128)(2,1)} %bitcast.5), calls=%async_computation | async-start | bytes 131072 | tf_op jit(solution)/shard_map/all_to_all | solution.py:31
  17.7 112.1 %reduce-scatter.2.cloned.1.call-start = ((), (), s32[]{:S(2)}) async-start(), calls=%async_computation.2 | async-start | bytes 2359296 | tf_op jit(solution)/shard_map/reduce_scatter | solution.py:56
  19.1 9.2 %copy-start.8 = (bf16[1024,512]{1,0:T(8,128)(2,1)S(1)}, bf16[1024,512]{1,0:T(8,128)(2,1)}, u32[]{:S(2)}) copy-start(bf16[1024,512]{1,0:T(8,128)(2,1)} %param.17) | copy-start | bytes 3145732
  28.4 2.0 copy-start.2
  42.2 4.3 %copy-start.10 = (s32[1,2048]{1,0:T(1,128)S(1)}, s32[1,2048]{1,0:T(1,128)}, u32[]{:S(2)}) copy-start(s32[1,2048]{1,0:T(1,128)} %param.13) | copy-start | bytes 24580
  46.5 8.2 %copy-start.5 = (f32[512,512]{1,0:T(8,128)S(1)}, f32[512,512]{1,0:T(8,128)}, u32[]{:S(2)}) copy-start(f32[512,512]{1,0:T(8,128)} %fusion.12) | copy-start | bytes 3145732
  46.5 8.2 %copy-start.9 = (bf16[1024,512]{1,0:T(8,128)(2,1)S(1)}, bf16[1024,512]{1,0:T(8,128)(2,1)}, u32[]{:S(2)}) copy-start(bf16[1024,512]{1,0:T(8,128)(2,1)} %param.17) | copy-start | bytes 3145732
  59.8 69.9 %copy-start.3 = (f32[1,128,512]{2,1,0:T(8,128)S(1)}, f32[1,128,512]{2,1,0:T(8,128)}, u32[]{:S(2)}) copy-start(f32[1,128,512]{2,1,0:T(8,128)} %param.18) | copy-start | bytes 786436
  59.9 190.2 %all-gather.3.cloned.1.call-start = ((), (), s32[]{:S(2)}) async-start(), calls=%async_computation.3 | async-start | bytes 4325376 | tf_op jit(solution)/shard_map/all_gather | solution.py:66
  254.7 1.1 copy-start.4
  255.4 1.2 copy-start.7
  255.8 0.8 copy-start.6
Sparse Core Ops, SparseCore 0:
  60.0 69.6 reduce-scatter.1
  190.9 59.1 all-gather.2
